TPU v7x, 32 devices: a whole 2x2x4 slice. The times are simulated.
32 devices in a mesh: dp: 4 (over y, x), mp: 8 (over z, core).
Axes of the slice: x: 2, y: 2, z: 4, core: 2. Of those that a mesh axis runs over, the one named last changes fastest.
Arguments:
- grads: bfloat16 [3, 8192, 28672], P(None, 'dp', 'mp'), may hold values from -8 to 8
- sketch: bfloat16 [28672, 256], P('mp'), may hold values from -0.03125 to 0.03125
- old_proj: bfloat16 [3, 8192, 256], P(None, 'dp'), may hold values from -0.0625 to 0.0625
- first_moment: float32 [3, 256, 28672], P(None, 'dp', 'mp'), may hold values from -12 to 12
- second_moment: float32 [3, 256, 28672], P(None, 'dp', 'mp'), may hold values from 0.25 to 4
- refresh_list: int32 [1], replicated, may hold values from 0 to 2
Outputs:
- new_first: float32 [3, 256, 28672], P(None, 'dp', 'mp')
- new_second: float32 [3, 256, 28672], P(None, 'dp', 'mp')
- direction: bfloat16 [3, 256, 28672], P(None, 'dp', 'mp')
All inputs are finite; a program needn't handle non-finite values.
Results may differ from a plain program's by a relative error of at most 0.0029.
Values sent between devices are 32-bit elements; how exact they have to be, the bound alone decides.
No kernel may reach another device: no remote copies, remote signals or barrier semaphores. Data moves between devices by JAX's collectives and lax.ppermute only.
A program may use at most 192 MiB of HBM per device.

v0:
```python
import jax
import jax.numpy as jnp
from jax import lax
from jax.sharding import PartitionSpec as P

first_decay = 0.9
second_decay = 0.95
epsilon = 1e-08
highest = lax.Precision.HIGHEST


def row_product(left, right):
    return lax.dot_general(
        left, right, (((0,), (0,)), ((), ())), precision=highest, preferred_element_type=jnp.float32
    )


def local(grads, sketch, old_proj, first_moment, second_moment, refresh_list):
    chosen = refresh_list[0]
    matrix_count = grads.shape[0]
    rank_rows = first_moment.shape[1]
    rank_total = sketch.shape[1]
    columns_total = sketch.shape[0] * lax.axis_size("mp")
    target = lax.dynamic_index_in_dim(grads, chosen, 0, keepdims=False)
    prior_proj = lax.dynamic_index_in_dim(old_proj, chosen, 0, keepdims=False).astype(jnp.float32)
    sketch_part = jnp.dot(target, sketch, preferred_element_type=jnp.float32)
    sketched = (lax.psum(sketch_part, "mp") / rank_total).astype(jnp.bfloat16)
    backward_part = lax.dot_general(
        target, sketched, (((0,), (0,)), ((), ())), preferred_element_type=jnp.float32
    )
    backward = (lax.psum(backward_part, "dp") / columns_total).astype(jnp.bfloat16)
    range_panel = lax.psum(jnp.dot(target, backward, preferred_element_type=jnp.float32), "mp")
    gram_part = row_product(range_panel, range_panel)
    gram_full = lax.psum(gram_part, "dp")
    factor = jnp.linalg.cholesky(gram_full)
    new_basis = jax.scipy.linalg.solve_triangular(factor, range_panel.T, lower=True).T
    turning = lax.psum(row_product(new_basis, prior_proj), "dp")
    picks = lax.broadcasted_iota(jnp.int32, (matrix_count, 1, 1), 0) == chosen
    projectors = jnp.where(picks, new_basis.astype(jnp.bfloat16)[None], old_proj)
    projected = jnp.transpose(
        lax.psum_scatter(
            jnp.einsum("kdr,kdc->rkc", projectors, grads, preferred_element_type=jnp.float32),
            "dp",
            scatter_dimension=0,
            tiled=True,
        ),
        (1, 0, 2),
    )
    first_own = lax.dynamic_index_in_dim(first_moment, chosen, 0, keepdims=False)
    second_own = lax.dynamic_index_in_dim(second_moment, chosen, 0, keepdims=False)
    own_start = lax.axis_index("dp") * rank_rows
    first_all, second_all = (
        lax.all_gather(first_own, "dp", axis=0, tiled=True),
        lax.all_gather(second_own, "dp", axis=0, tiled=True),
    )
    own_turning = lax.dynamic_slice_in_dim(turning, own_start, rank_rows, 0)
    turned_first = jnp.dot(own_turning, first_all, precision=highest)
    turned_second = jnp.dot(own_turning * own_turning, second_all, precision=highest)
    moved_first = jnp.where(picks, turned_first[None], first_moment)
    moved_second = jnp.where(picks, turned_second[None], second_moment)
    updated_first = first_decay * moved_first + (1.0 - first_decay) * projected
    updated_second = second_decay * moved_second + (1.0 - second_decay) * projected * projected
    direction = (updated_first / (jnp.sqrt(updated_second) + epsilon)).astype(jnp.bfloat16)
    return (updated_first, updated_second, direction)


def solution(mesh):
    placed = (
        P(None, "dp", "mp"),
        P("mp", None),
        P(None, "dp", None),
        P(None, "dp", "mp"),
        P(None, "dp", "mp"),
        P(),
    )
    return jax.shard_map(
        local,
        mesh=mesh,
        in_specs=placed,
        out_specs=(P(None, "dp", "mp"), P(None, "dp", "mp"), P(None, "dp", "mp")),
        check_vma=False,
    )
```

profile of v0, /device:TPU:0, one launch (start us, length us, event | category | flops | bytes accessed | tf_op | source)
XLA Modules:
  0.0 609.4 jit_solution(3067259670049275815)
XLA Ops:
  8.7 8.6 %fusion.4 = f32[2048,256]{1,0:T(8,128)} fusion(bf16[3584,256]{1,0:T(8,128)(2,1)S(1)} %copy-done, bf16[3,2048,3584]{2,1,0:T(8,128)(2,1)} %param.6, s32[]{:T(128)S(6)} %select_n.27), kind=kOutput, calls=%fused_computation.6 | convolution fusion | flops 3758096384 | bytes 18612228 | tf_op jit(solution)/shard_map/dot_general | solution.py:26
  17.3 68.0 %all-reduce.7.cloned.1.call-done = f32[2048,256]{1,0:T(8,128)} async-done(((f32[2048,256]{1,0:T(8,128)}), f32[2048,256]{1,0:T(8,128)}) %all-reduce.7.cloned.1.call-update) | async-done | bytes 2097168 | tf_op jit(solution)/shard_map/psum | solution.py:27
  85.3 11.6 %fusion.2 = f32[3584,256]{1,0:T(8,128)} fusion(bf16[3,2048,3584]{2,1,0:T(8,128)(2,1)} %param.6, s32[]{:T(128)S(6)} %select_n.27, f32[2048,256]{1,0:T(8,128)} %all-reduce.7.cloned.1.call-done), kind=kOutput, calls=%fused_computation.4 | convolution fusion | flops 3759144960 | bytes 20447236 | tf_op jit(solution)/shard_map/dot_general | solution.py:28
  97.0 95.4 %all-reduce.9.cloned.1.call-done = f32[3584,256]{1,0:T(8,128)} async-done(((f32[3584,256]{1,0:T(8,128)}), f32[3584,256]{1,0:T(8,128)}) %all-reduce.9.cloned.1.call-update) | async-done | bytes 3670032 | tf_op jit(solution)/shard_map/psum | solution.py:31
  192.4 11.5 %fusion = f32[2048,256]{1,0:T(8,128)} fusion(bf16[3,2048,3584]{2,1,0:T(8,128)(2,1)} %param.6, s32[]{:T(128)S(6)} %select_n.27, f32[3584,256]{1,0:T(8,128)} %all-reduce.9.cloned.1.call-done), kind=kOutput, calls=%fused_computation.2 | convolution fusion | flops 3759931392 | bytes 20447236 | tf_op jit(solution)/shard_map/dot_general | solution.py:32
  204.4 64.7 %all-reduce.11.cloned.1.call-done = f32[2048,256]{1,0:T(8,128)} async-done(((f32[2048,256]{1,0:T(8,128)}), f32[2048,256]{1,0:T(8,128)}) %all-reduce.11.cloned.1.call-update) | async-done | bytes 2097168 | tf_op jit(solution)/shard_map/psum | solution.py:32
  269.2 6.4 %fusion.48 = f32[256,256]{0,1:T(8,128)} fusion(f32[2048,256]{1,0:T(8,128)} %all-reduce.11.cloned.1.call-done), kind=kOutput, calls=%fused_computation.75 | convolution fusion | flops 1610612736 | bytes 2359296 | tf_op jit(solution)/shard_map/dot_general | solution.py:13
  275.6 2.2 constant_dynamic-slice_fusion.1
  277.9 40.5 %all-reduce.13.cloned.1.call-done = f32[256,256]{0,1:T(8,128)} async-done(((f32[256,256]{0,1:T(8,128)}), f32[256,256]{0,1:T(8,128)}) %all-reduce.13.cloned.1.call-update) | async-done | bytes 262160 | tf_op jit(solution)/shard_map/psum | solution.py:34
  320.5 11.7 %cholesky.50 = f32[128,128]{1,0:T(8,128)S(1)} custom-call(f32[128,128]{1,0:T(8,128)S(1)} %cholesky.118), custom_call_target="Cholesky" | custom-call | tf_op jit(solution)/shard_map/jit(cholesky)/cholesky | solution.py:35
  332.2 9.8 %custom-call.15 = f32[1,128,128]{1,2,0:T(8,128)S(1)} custom-call(f32[1,128,128]{2,1,0:T(8,128)S(1)} %get-tuple-element.27), custom_call_target="InvertDiagBlocksLowerTriangular" | custom-call | tf_op jit(solution)/shard_map/jit(cholesky)/cholesky | solution.py:35
  342.5 11.7 %cholesky.105 = f32[128,128]{1,0:T(8,128)S(1)} custom-call(f32[128,128]{1,0:T(8,128)S(1)} %convolution_subtract_fusion.1), custom_call_target="Cholesky" | custom-call | tf_op jit(solution)/shard_map/jit(cholesky)/cholesky | solution.py:35
  356.5 4.2 while.1
  360.7 19.7 %custom-call.16 = f32[2,128,128]{1,2,0:T(8,128)S(1)} custom-call(f32[2,128,128]{2,1,0:T(8,128)S(1)} %get-tuple-element.10), custom_call_target="InvertDiagBlocksLowerTriangular" | custom-call | tf_op jit(solution)/shard_map/jit(_solve_triangular)/triangular_solve | solution.py:36
  380.4 2.3 fusion.22
  382.7 3.0 convolution_subtract_fusion
  386.8 3.0 fusion.19
  395.0 24.7 %convolution_bitcast_fusion = f32[256,3,3584]{2,0,1:T(8,128)} fusion(bf16[3,2048,3584]{2,1,0:T(8,128)(2,1)} %param.6, bf16[3,2048,256]{2,1,0:T(8,128)(2,1)} %param.8, pred[3]{0:T(512)(128)(4,1)S(1)} %iota_compare_fusion.3, bf16[2048,256]{1,0:T(8,128)(2,1)S(1)} %copy.11), kind=kOutput, calls=%fused_computation.11 | convolution fusion | flops 11275862016 | bytes 59244548 | tf_op jit(solution)/shard_map/kdr,kdc->rkc/dot_general | solution.py:42
  419.8 13.3 %all-reduce.15.cloned.1.call-done = f32[256,256]{1,0:T(8,128)} async-done(((f32[256,256]{1,0:T(8,128)}), f32[256,256]{1,0:T(8,128)}) %all-reduce.15.cloned.1.call-update) | async-done | bytes 262160 | tf_op jit(solution)/shard_map/psum | solution.py:37
  433.0 4.4 fusion.9
  437.4 46.3 %all-gather.5.cloned.1.call-done = f32[1,256,3584]{2,1,0:T(8,128)} async-done(((f32[1,64,3584]{2,1,0:T(8,128)}), f32[1,256,3584]{2,1,0:T(8,128)}) %all-gather.5.cloned.1.call-update) | async-done | bytes 3670032 | tf_op jit(solution)/shard_map/all_gather | solution.py:53
  483.7 5.3 fusion.11
  489.0 105.6 %reduce-scatter.2.cloned.1.call-done = f32[64,3,3584]{2,0,1:T(8,128)} async-done(((f32[256,3,3584]{2,0,1:T(8,128)}), f32[64,3,3584]{2,0,1:T(8,128)}) %reduce-scatter.2.cloned.1.call-update) | async-done | bytes 2752528 | tf_op jit(solution)/shard_map/reduce_scatter | solution.py:41
  594.6 7.8 %divide_convert_fusion = (bf16[3,64,3584]{2,1,0:T(8,128)(2,1)}, f32[3,64,3584]{2,1,0:T(8,128)}, f32[3,64,3584]{2,1,0:T(8,128)}) fusion(f32[64,3,3584]{2,0,1:T(8,128)} %reduce-scatter.2.cloned.1.call-done, f32[3,64,3584]{2,1,0:T(8,128)} %param.10, f32[64,3584]{1,0:T(8,128)S(1)} %fusion.9, pred[3]{0:T(512)(128)(4,1)S(1)} %iota_compare_fusion.3, ...), kind=kLoop, calls=%fused_computation.23 | loop fusion | flops 8257536 | bytes 16973828 | tf_op jit(solution)/shard_map/convert_element_type | solution.py:63
  (45 shorter events, 15.2 us)
Async XLA Ops:
  7.2 1.5 copy-start
  7.2 78.1 %all-reduce.7.cloned.1.call-start = ((), (), s32[]{:S(2)}) async-start(), calls=%async_computation.1 | async-start | bytes 4194304 | tf_op jit(solution)/shard_map/psum | solution.py:27
  17.3 175.1 %all-reduce.9.cloned.1.call-start = ((), (), s32[]{:S(2)}) async-start(), calls=%async_computation.2 | async-start | bytes 7340032 | tf_op jit(solution)/shard_map/psum | solution.py:31
  96.9 172.2 %all-reduce.11.cloned.1.call-start = ((), (), s32[]{:S(2)}) async-start(), calls=%async_computation.3 | async-start | bytes 4194304 | tf_op jit(solution)/shard_map/psum | solution.py:32
  203.9 114.4 %all-reduce.13.cloned.1.call-start = ((), (), s32[]{:S(2)}) async-start(), calls=%async_computation.4 | async-start | bytes 524288 | tf_op jit(solution)/shard_map/psum | solution.py:34
  275.6 144.2 %all-gather.7.cloned.1.call-start = ((), (), s32[]{:S(2)}) async-start(), calls=%async_computation.8 | async-start | bytes 4587520 | tf_op jit(solution)/shard_map/all_gather | solution.py:54
  277.8 155.2 %all-reduce.15.cloned.1.call-start = ((), (), s32[]{:S(2)}) async-start(), calls=%async_computation.5 | async-start | bytes 524288 | tf_op jit(solution)/shard_map/psum | solution.py:37
  389.9 93.8 %all-gather.5.cloned.1.call-start = ((), (), s32[]{:S(2)}) async-start(), calls=%async_computation.7 | async-start | bytes 4587520 | tf_op jit(solution)/shard_map/all_gather | solution.py:53
  392.1 202.5 %reduce-scatter.2.cloned.1.call-start = ((), (), s32[]{:S(2)}) async-start(), calls=%async_computation.6 | async-start | bytes 13762560 | tf_op jit(solution)/shard_map/reduce_scatter | solution.py:41
  594.6 7.8 %copy-start.1 = (bf16[3584,256]{1,0:T(8,128)(2,1)S(1)}, bf16[3584,256]{1,0:T(8,128)(2,1)}, u32[]{:S(2)}) copy-start(bf16[3584,256]{1,0:T(8,128)(2,1)} %param.7) | copy-start | bytes 5505028
Sparse Core Ops, SparseCore 0:
  17.4 67.8 all-reduce.6
  97.0 95.2 all-reduce.8
  204.1 65.0 all-reduce.10
  275.7 42.6 all-reduce.12
  320.6 48.3 all-gather.6
  390.0 43.0 all-reduce.14
  435.5 48.1 all-gather.4
  486.8 107.7 reduce-scatter.1
where the time goes:
time: 617 us; the launch traced here: 609 us
  waiting for transfers between devices  434 us (70%)
  matrix products  82.4 us (13%)
  other arithmetic  63.6 us (10%)
  between operations  16.6 us (3%)
  local copies, waits for them, and re-layouts  11.9 us (2%)
    reduce_scatter x1, waiting for transfers between devices, local(): lax.psum_scatter(jnp.einsum('kdr,kdc->rkc', projectors, grads, preferred_...  106 us
    psum x1, waiting for transfers between devices, local(): lax.psum(backward_part, 'dp') / columns_total  95.4 us
    psum x1, waiting for transfers between devices, local(): sketched = (lax.psum(sketch_part, 'mp') / rank_total).astype(jnp.bfloat16)  68 us
    psum x1, waiting for transfers between devices, local(): lax.psum(jnp.dot(target, backward, preferred_element_type=jnp.float32), '...  64.7 us
    all_gather x1, waiting for transfers between devices, local(): lax.all_gather(first_own, 'dp', axis=0, tiled=True)  46.3 us
    psum x1, waiting for transfers between devices, local(): gram_full = lax.psum(gram_part, 'dp')  40.5 us
    another operation x6, other arithmetic, local(): factor = jnp.linalg.cholesky(gram_full)  34 us
    dot_general x1, matrix products, local(): jnp.einsum('kdr,kdc->rkc', projectors, grads, preferred_element_type=jnp....  24.7 us
  transfers between devices with their start and end apart: 8, of which 7 were waited for; matrix products, arithmetic and copies ran while one was open for 18% of the time, Pallas kernels for 0%

commit v1 on v0

--- a/solution.py
+++ b/solution.py
@@ -7,6 +7,18 @@
 second_decay = 0.95
 epsilon = 1e-08
 highest = lax.Precision.HIGHEST
+
+
+def collect(value, axis, dim):
+    ways, here, lap = (lax.axis_size(axis), lax.axis_index(axis), value.shape[dim])
+    line, have = (value, 1)
+    while have < ways:
+        line = jnp.concatenate(
+            [line, lax.ppermute(line, axis, [(d, (d - have) % ways) for d in range(ways)])],
+            axis=dim,
+        )
+        have = 2 * have
+    return jnp.roll(line, here * lap, axis=dim)
 
 
 def row_product(left, right):
@@ -50,7 +62,7 @@
     second_own = lax.dynamic_index_in_dim(second_moment, chosen, 0, keepdims=False)
     own_start = lax.axis_index("dp") * rank_rows
     first_all, second_all = (
-        lax.all_gather(first_own, "dp", axis=0, tiled=True),
+        collect(first_own, "dp", 0),
         lax.all_gather(second_own, "dp", axis=0, tiled=True),
     )
     own_turning = lax.dynamic_slice_in_dim(turning, own_start, rank_rows, 0)

time: 617 us -> 651 us (1.055)
  waiting for transfers between devices: 434 us -> 455 us
  local copies, waits for them, and re-layouts: 11.9 us -> 20.7 us
    ppermute x0 -> x2, waiting for transfers between devices: none -> 82.2 us  [collect(): lax.ppermute(line, axis, [(d, (d - have) % ways) for d in range(ways)])]
    all_gather x1 -> x0, waiting for transfers between devices: 46.3 us -> none  [local(): lax.all_gather(first_own, 'dp', axis=0, tiled=True)]
    psum x1, waiting for transfers between devices: 13.3 us -> 0.01 us  [local(): turning = lax.psum(row_product(new_basis, prior_proj), 'dp')]
    unnamed x4 -> x9, local copies, waits for them, and re-layouts: 0.7 us -> 8.87 us
  transfers between devices with their start and end apart: 8 -> 9, of which waited for: 7 -> 7; matrix products, arithmetic and copies ran while one was open for 18% -> 8% of each run, Pallas kernels for 0% -> 0%
where the time goes in v1:
time: 651 us; the launch traced here: 643 us
  waiting for transfers between devices  455 us (70%)
  matrix products  82.4 us (13%)
  other arithmetic  65 us (10%)
  local copies, waits for them, and re-layouts  20.7 us (3%)
  between operations  16.6 us (3%)
    reduce_scatter x1, waiting for transfers between devices, local(): lax.psum_scatter(jnp.einsum('kdr,kdc->rkc', projectors, grads, preferred_...  102 us
    psum x1, waiting for transfers between devices, local(): lax.psum(backward_part, 'dp') / columns_total  95.4 us
    ppermute x2, waiting for transfers between devices, collect(): lax.ppermute(line, axis, [(d, (d - have) % ways) for d in range(ways)])  82.2 us
    psum x1, waiting for transfers between devices, local(): sketched = (lax.psum(sketch_part, 'mp') / rank_total).astype(jnp.bfloat16)  68 us
    psum x1, waiting for transfers between devices, local(): lax.psum(jnp.dot(target, backward, preferred_element_type=jnp.float32), '...  64.7 us
    psum x1, waiting for transfers between devices, local(): gram_full = lax.psum(gram_part, 'dp')  42.7 us
    another operation x6, other arithmetic, local(): factor = jnp.linalg.cholesky(gram_full)  34 us
    dot_general x1, matrix products, local(): jnp.einsum('kdr,kdc->rkc', projectors, grads, preferred_element_type=jnp....  24.7 us
  transfers between devices with their start and end apart: 9, of which 7 were waited for; matrix products, arithmetic and copies ran while one was open for 8% of the time, Pallas kernels for 0%

profile of v1, /device:TPU:0, one launch (start us, length us, event | category | flops | bytes accessed | tf_op | source)
XLA Modules:
  0.0 643.4 jit_solution(11607018151543322104)
XLA Ops:
  8.7 8.6 %fusion.4 = f32[2048,256]{1,0:T(8,128)} fusion(bf16[3584,256]{1,0:T(8,128)(2,1)S(1)} %copy-done, bf16[3,2048,3584]{2,1,0:T(8,128)(2,1)} %param.6, s32[]{:T(128)S(6)} %select_n.40), kind=kOutput, calls=%fused_computation.6 | convolution fusion | flops 3758096384 | bytes 18612228 | tf_op jit(solution)/shard_map/dot_general | solution.py:38
  17.3 68.0 %all-reduce.7.cloned.1.call-done = f32[2048,256]{1,0:T(8,128)} async-done(((f32[2048,256]{1,0:T(8,128)}), f32[2048,256]{1,0:T(8,128)}) %all-reduce.7.cloned.1.call-update) | async-done | bytes 2097168 | tf_op jit(solution)/shard_map/psum | solution.py:39
  85.3 11.6 %fusion.2 = f32[3584,256]{1,0:T(8,128)} fusion(bf16[3,2048,3584]{2,1,0:T(8,128)(2,1)} %param.6, s32[]{:T(128)S(6)} %select_n.40, f32[2048,256]{1,0:T(8,128)} %all-reduce.7.cloned.1.call-done), kind=kOutput, calls=%fused_computation.4 | convolution fusion | flops 3759144960 | bytes 20447236 | tf_op jit(solution)/shard_map/dot_general | solution.py:40
  97.0 95.4 %all-reduce.9.cloned.1.call-done = f32[3584,256]{1,0:T(8,128)} async-done(((f32[3584,256]{1,0:T(8,128)}), f32[3584,256]{1,0:T(8,128)}) %all-reduce.9.cloned.1.call-update) | async-done | bytes 3670032 | tf_op jit(solution)/shard_map/psum | solution.py:43
  192.4 11.5 %fusion = f32[2048,256]{1,0:T(8,128)} fusion(bf16[3,2048,3584]{2,1,0:T(8,128)(2,1)} %param.6, s32[]{:T(128)S(6)} %select_n.40, f32[3584,256]{1,0:T(8,128)} %all-reduce.9.cloned.1.call-done), kind=kOutput, calls=%fused_computation.2 | convolution fusion | flops 3759931392 | bytes 20447236 | tf_op jit(solution)/shard_map/dot_general | solution.py:44
  204.4 64.7 %all-reduce.11.cloned.1.call-done = f32[2048,256]{1,0:T(8,128)} async-done(((f32[2048,256]{1,0:T(8,128)}), f32[2048,256]{1,0:T(8,128)}) %all-reduce.11.cloned.1.call-update) | async-done | bytes 2097168 | tf_op jit(solution)/shard_map/psum | solution.py:44
  269.2 6.4 fusion.48
  275.6 42.7 %all-reduce.13.cloned.1.call-done = f32[256,256]{0,1:T(8,128)} async-done(((f32[256,256]{0,1:T(8,128)}), f32[256,256]{0,1:T(8,128)}) %all-reduce.13.cloned.1.call-update) | async-done | bytes 262160 | tf_op jit(solution)/shard_map/psum | solution.py:46
  320.5 11.7 %cholesky.50 = f32[128,128]{1,0:T(8,128)S(1)} custom-call(f32[128,128]{1,0:T(8,128)S(1)} %cholesky.118), custom_call_target="Cholesky" | custom-call | tf_op jit(solution)/shard_map/jit(cholesky)/cholesky | solution.py:47
  332.2 9.8 %custom-call.15 = f32[1,128,128]{1,2,0:T(8,128)S(1)} custom-call(f32[1,128,128]{2,1,0:T(8,128)S(1)} %get-tuple-element.29), custom_call_target="InvertDiagBlocksLowerTriangular" | custom-call | tf_op jit(solution)/shard_map/jit(cholesky)/cholesky | solution.py:47
  342.5 11.7 %cholesky.105 = f32[128,128]{1,0:T(8,128)S(1)} custom-call(f32[128,128]{1,0:T(8,128)S(1)} %convolution_subtract_fusion.1), custom_call_target="Cholesky" | custom-call | tf_op jit(solution)/shard_map/jit(cholesky)/cholesky | solution.py:47
  356.3 4.2 while.1
  360.5 19.7 %custom-call.16 = f32[2,128,128]{1,2,0:T(8,128)S(1)} custom-call(f32[2,128,128]{2,1,0:T(8,128)S(1)} %get-tuple-element.10), custom_call_target="InvertDiagBlocksLowerTriangular" | custom-call | tf_op jit(solution)/shard_map/jit(_solve_triangular)/triangular_solve | solution.py:48
  382.5 3.0 convolution_subtract_fusion
  386.6 3.0 fusion.19
  394.7 24.7 %convolution_bitcast_fusion = f32[256,3,3584]{2,0,1:T(8,128)} fusion(bf16[3,2048,3584]{2,1,0:T(8,128)(2,1)} %param.6, bf16[3,2048,256]{2,1,0:T(8,128)(2,1)} %param.8, pred[3]{0:T(512)(128)(4,1)S(1)} %iota_compare_fusion.3, bf16[2048,256]{1,0:T(8,128)(2,1)S(1)} %copy.11), kind=kOutput, calls=%fused_computation.11 | convolution fusion | flops 11275862016 | bytes 59244548 | tf_op jit(solution)/shard_map/kdr,kdc->rkc/dot_general | solution.py:54
  423.3 21.5 %collective-permute-done = f32[64,3584]{1,0:T(8,128)S(1)} collective-permute-done((f32[64,3584]{1,0:T(8,128)S(1)}, f32[64,3584]{1,0:T(8,128)S(1)}, u32[]{:S(2)}, u32[]{:S(2)}) %collective-permute-start) | collective-permute-done | bytes 917536 | tf_op jit(solution)/shard_map/ppermute | solution.py:17
  448.6 60.6 %collective-permute-done.1 = f32[128,3584]{1,0:T(8,128)} collective-permute-done((f32[128,3584]{1,0:T(8,128)}, f32[128,3584]{1,0:T(8,128)}, u32[]{:S(2)}, u32[]{:S(2)}) %collective-permute-start.1) | collective-permute-done | bytes 1835040 | tf_op jit(solution)/shard_map/ppermute | solution.py:17
  509.2 2.9 constant_dynamic-update-slice_fusion.3
  514.0 2.9 constant_dynamic-update-slice_fusion
  516.9 4.4 fusion.11
  521.3 5.3 fusion.9
  526.7 101.8 %reduce-scatter.2.cloned.1.call-done = f32[64,3,3584]{2,0,1:T(8,128)} async-done(((f32[256,3,3584]{2,0,1:T(8,128)}), f32[64,3,3584]{2,0,1:T(8,128)}) %reduce-scatter.2.cloned.1.call-update) | async-done | bytes 2752528 | tf_op jit(solution)/shard_map/reduce_scatter | solution.py:53
  628.5 7.9 %divide_convert_fusion = (bf16[3,64,3584]{2,1,0:T(8,128)(2,1)}, f32[3,64,3584]{2,1,0:T(8,128)}, f32[3,64,3584]{2,1,0:T(8,128)}) fusion(f32[64,3,3584]{2,0,1:T(8,128)} %reduce-scatter.2.cloned.1.call-done, f32[3,64,3584]{2,1,0:T(8,128)} %param.10, f32[64,3584]{1,0:T(8,128)} %fusion.9, pred[3]{0:T(512)(128)(4,1)S(1)} %iota_compare_fusion.3, ...), kind=kLoop, calls=%fused_computation.23 | loop fusion | flops 8257536 | bytes 16973828 | tf_op jit(solution)/shard_map/convert_element_type | solution.py:75
  (52 shorter events, 26.7 us)
Async XLA Ops:
  7.2 1.5 copy-start
  7.2 78.1 %all-reduce.7.cloned.1.call-start = ((), (), s32[]{:S(2)}) async-start(), calls=%async_computation.1 | async-start | bytes 4194304 | tf_op jit(solution)/shard_map/psum | solution.py:39
  17.3 175.1 %all-reduce.9.cloned.1.call-start = ((), (), s32[]{:S(2)}) async-start(), calls=%async_computation.2 | async-start | bytes 7340032 | tf_op jit(solution)/shard_map/psum | solution.py:43
  96.9 172.2 %all-reduce.11.cloned.1.call-start = ((), (), s32[]{:S(2)}) async-start(), calls=%async_computation.3 | async-start | bytes 4194304 | tf_op jit(solution)/shard_map/psum | solution.py:44
  203.9 114.4 %all-reduce.13.cloned.1.call-start = ((), (), s32[]{:S(2)}) async-start(), calls=%async_computation.4 | async-start | bytes 524288 | tf_op jit(solution)/shard_map/psum | solution.py:46
  275.6 241.4 %all-reduce.15.cloned.1.call-start = ((), (), s32[]{:S(2)}) async-start(), calls=%async_computation.5 | async-start | bytes 524288 | tf_op jit(solution)/shard_map/psum | solution.py:49
  389.6 131.7 %all-gather.3.cloned.1.call-start = ((), (), s32[]{:S(2)}) async-start(), calls=%async_computation.7 | async-start | bytes 4587520 | tf_op jit(solution)/shard_map/all_gather | solution.py:66
  391.9 236.6 %reduce-scatter.2.cloned.1.call-start = ((), (), s32[]{:S(2)}) async-start(), calls=%async_computation.6 | async-start | bytes 13762560 | tf_op jit(solution)/shard_map/reduce_scatter | solution.py:53
  421.8 23.0 %collective-permute-start = (f32[64,3584]{1,0:T(8,128)S(1)}, f32[64,3584]{1,0:T(8,128)S(1)}, u32[]{:S(2)}, u32[]{:S(2)}) collective-permute-start(f32[64,3584]{1,0:T(8,128)S(1)} %get-tuple-element.23), channel_id=1, source_target_pairs={{0,24},{8,0},{16,8},{24,16},{1,25},{9,1},{17,9},{25,17},{2,26},{10... | collective-permute-start | bytes 2752520 | tf_op jit(solution)/shard_map/ppermute | solution.py:17
  446.2 63.0 %collective-permute-start.1 = (f32[128,3584]{1,0:T(8,128)}, f32[128,3584]{1,0:T(8,128)}, u32[]{:S(2)}, u32[]{:S(2)}) collective-permute-start(f32[128,3584]{1,0:T(8,128)} %pad_maximum_fusion.1), channel_id=1, source_target_pairs={{0,16},{8,24},{16,0},{24,8},{1,17},{9,25},{17,1},{25,9},{2,18},{10... | collective-permute-start | bytes 5505032 | tf_op jit(solution)/shard_map/ppermute | solution.py:17
  628.5 7.9 %copy-start.1 = (bf16[3584,256]{1,0:T(8,128)(2,1)S(1)}, bf16[3584,256]{1,0:T(8,128)(2,1)}, u32[]{:S(2)}) copy-start(bf16[3584,256]{1,0:T(8,128)(2,1)} %param.7) | copy-start | bytes 5505028
Sparse Core Ops, SparseCore 0:
  17.4 67.8 all-reduce.6
  97.0 95.2 all-reduce.8
  204.1 65.0 all-reduce.10
  275.7 42.6 all-reduce.12
  389.8 43.2 all-reduce.14
  435.3 81.2 all-gather.2
  519.7 108.6 reduce-scatter.1
